TPU v7x, 512 devices: a whole 4x4x16 slice. The times are simulated.
512 devices in a mesh: row: 32 (over z, core), col: 16 (over y, x).
Axes of the slice: x: 4, y: 4, z: 16, core: 2. Of those that a mesh axis runs over, the one named last changes fastest.
Arguments:
- train_points: float32 [64, 32768], P(None, ('row', 'col')), may hold values from -6 to 6
- cand_points: float32 [64, 32768], P(None, ('row', 'col')), may hold values from -6 to 6
- inv_length: float32 [64], replicated, may hold values from 0.04 to 0.7
- noise: float32 [32768], P(('row', 'col')), may hold values from 0.5 to 4
- targets: float32 [16, 32768], P(None, ('row', 'col')), may hold values from -15 to 15
Outputs:
- solution: float32 [16, 32768], P(None, ('row', 'col'))
- post_mean: float32 [16, 32768], P(None, ('row', 'col'))
All inputs are finite; a program needn't handle non-finite values.
Results may differ from a plain program's by a relative error of at most 0.0047.
Values may be sent and summed in bfloat16 or wider, within the bound.
No kernel may reach another device: no remote copies, remote signals or barrier semaphores. Data moves between devices by JAX's collectives and lax.ppermute only.
A program may use at most 64 MiB of HBM per device.

v0:
```python
import math
import jax
import jax.numpy as jnp
from jax import lax
from jax.sharding import PartitionSpec as P

ITERS = 2
root_five = math.sqrt(5.0)


def matern(left, left_norm, right, right_norm):
    inner = lax.dot_general(
        left, right, (((0,), (0,)), ((), ())), preferred_element_type=jnp.float32
    )
    dist_sq = jnp.maximum(left_norm[:, None] + right_norm[None, :] - 2.0 * inner, 0.0)
    radius = jnp.sqrt(dist_sq)
    return (1.0 + root_five * radius + 5.0 / 3.0 * dist_sq) * jnp.exp(-root_five * radius)


def tile_rows(amount):
    best = 1
    for candidate in range(1, 513):
        if amount % candidate == 0:
            best = candidate
    return best


def accumulate(carried, vector_piece, piece_points, piece_norms, other, other_norms):
    amount = vector_piece.shape[1]
    block = tile_rows(amount)

    def advance(block_index, running):
        offset = block_index * block
        sub_points = lax.dynamic_slice_in_dim(piece_points, offset, block, 1)
        sub_norms = lax.dynamic_slice_in_dim(piece_norms, offset, block, 0)
        sub_vector = lax.dynamic_slice_in_dim(vector_piece, offset, block, 1)
        kernel_tile = matern(sub_points, sub_norms, other, other_norms)
        return running + jnp.dot(
            sub_vector,
            kernel_tile,
            precision=lax.Precision.HIGHEST,
            preferred_element_type=jnp.float32,
        )

    return lax.fori_loop(0, amount // block, advance, carried)


def per_device(train_points, cand_points, inv_length, noise, targets):
    scaled_train = (train_points * inv_length[:, None]).astype(jnp.bfloat16)
    scaled_cand = (cand_points * inv_length[:, None]).astype(jnp.bfloat16)
    row_train, row_cand = (
        lax.all_gather(scaled_train, "col", axis=1, tiled=True),
        lax.all_gather(scaled_cand, "col", axis=1, tiled=True),
    )
    col_train = lax.all_gather(scaled_train, "row", axis=1, tiled=True)
    row_norms = jnp.sum(jnp.square(row_train.astype(jnp.float32)), axis=0)
    cand_norms = jnp.sum(jnp.square(row_cand.astype(jnp.float32)), axis=0)
    col_norms = jnp.sum(jnp.square(col_train.astype(jnp.float32)), axis=0)
    outputs = targets.shape[0]

    def from_columns(other, other_norms, carried, vector_piece):
        return accumulate(carried, vector_piece, col_train, col_norms, other, other_norms)

    def squares(residual):
        return lax.psum(jnp.sum(residual * residual, axis=1), ("row", "col"))

    solution = jnp.zeros_like(targets)
    residual = targets
    direction = targets
    norm_now = squares(residual)
    for iteration in range(ITERS):
        start_total = jnp.zeros((outputs, row_train.shape[1]), jnp.float32)
        partial_image = from_columns(
            row_train, row_norms, start_total, lax.all_gather(direction, "row", axis=1, tiled=True)
        )
        own_image = lax.psum_scatter(partial_image, "col", scatter_dimension=1, tiled=True)
        image = own_image + noise[None, :] * direction
        alpha = norm_now / lax.psum(jnp.sum(direction * image, axis=1), ("row", "col"))
        solution = solution + alpha[:, None] * direction
        residual = residual - alpha[:, None] * image
        norm_next = squares(residual)
        direction = residual + (norm_next / norm_now)[:, None] * direction
        norm_now = norm_next
    mean_start = jnp.zeros((outputs, row_cand.shape[1]), jnp.float32)
    partial_mean = from_columns(
        row_cand, cand_norms, mean_start, lax.all_gather(solution, "row", axis=1, tiled=True)
    )
    post_mean = lax.psum_scatter(partial_mean, "col", scatter_dimension=1, tiled=True)
    return (solution, post_mean)


def solution(mesh):
    placed = (
        P(None, ("row", "col")),
        P(None, ("row", "col")),
        P(),
        P(("row", "col")),
        P(None, ("row", "col")),
    )
    return jax.shard_map(
        per_device,
        mesh=mesh,
        in_specs=placed,
        out_specs=(P(None, ("row", "col")), P(None, ("row", "col"))),
        check_vma=False,
    )
```

profile of v0, /device:TPU:2, one launch (start us, length us, event | category | flops | bytes accessed | tf_op | source)
XLA Modules:
  0.0 763.7 jit_solution(8951887657408759057)
XLA Ops:
  7.2 0.8 copy.22
  8.1 0.8 copy.29
  8.9 0.7 multiply_convert_fusion
  9.6 37.6 %all_gather.19 = bf16[64,2048]{0,1:T(8,128)(2,1)S(1)} all-gather(bf16[64,64]{0,1:T(8,128)(2,1)S(1)} %get-tuple-element.538), channel_id=1, replica_groups=mesh['row'=32,'col'=16] {'row'}, dimensions={1}, use_global_device_ids=true | all-gather | bytes 270336 | tf_op jit(solution)/shard_map/all_gather | solution.py:55
  47.2 0.2 copy.23
  47.4 0.3 multiply_reduce_fusion
  47.8 23.8 %all_gather.20 = bf16[64,1024]{0,1:T(8,128)(2,1)S(1)} all-gather(bf16[64,64]{0,1:T(8,128)(2,1)S(1)} %get-tuple-element.538), channel_id=1, replica_groups=mesh['row'=32,'col'=16] {'col'}, dimensions={1}, use_global_device_ids=true | all-gather | bytes 139264 | tf_op jit(solution)/shard_map/all_gather | solution.py:52
  71.5 0.1 copy.24
  71.7 0.2 multiply_reduce_fusion.2
  71.9 27.5 %all-gather = f32[32,64,16]{1,2,0:T(8,128)S(1)} all-gather(f32[1,64,16]{1,2,0:T(8,128)S(1)} %bitcast.37), channel_id=1, replica_groups=mesh['row'=32,'col'=16] {'row'}, dimensions={0}, use_global_device_ids=true | all-gather | bytes 135168 | tf_op jit(solution)/shard_map/all_gather | solution.py:74
  99.4 0.1 copy.21
  99.5 0.1 reshape.16
  99.6 11.9 %while.42 = (s32[]{:T(128)}, f32[16,1024]{1,0:T(8,128)S(1)}, f32[16,2048]{1,0:T(8,128)S(1)}, f32[2048]{0:T(1024)S(1)}, f32[1024]{0:T(1024)S(1)}, /*index=5*/bf16...) while((s32[]{:T(128)}, f32[16,1024]{1,0:T(8,128)S(1)}, ...), condition=%wide.region_5.0_spmd.clone, body=%wide.region_4.0_spmd.clone.sunk | while | flops 173047808 | bytes 4565169 | solution.py:45
  99.7 0.5 fusion.131
  100.1 0.1 dynamic_slice.95
  100.2 2.4 fusion.132
  102.6 0.5 fusion.131
  103.2 2.4 fusion.132
  105.6 0.5 fusion.131
  106.1 2.4 fusion.132
  108.6 0.5 fusion.131
  109.1 2.4 fusion.132
  111.6 1.0 copy.32
  112.6 83.7 %reduce-scatter.10.cloned.1.call-done = f32[64,16]{1,0:T(8,128)} async-done(((f32[1024,16]{1,0:T(8,128)}), f32[64,16]{1,0:T(8,128)}) %reduce-scatter.10.cloned.1.call-update) | async-done | bytes 4112
  196.4 0.8 copy.33
  197.2 0.1 multiply_reduce_fusion.5
  197.3 101.8 %all-reduce = (f32[16]{0:T(128)S(1)}, f32[16]{0:T(128)S(1)}) all-reduce(f32[16]{0:T(128)S(1)} %get-tuple-element.492, f32[16]{0:T(128)S(1)} %get-tuple-element.491), channel_id=1, replica_groups=mesh['row'=32,'col'=16] {'row','col'}, use_global_device_ids=true, to_apply=%region_1.0 | all-reduce | flops 32 | bytes 256 | tf_op jit(solution)/shard_map/psum | solution.py:65
  299.2 0.2 multiply_reduce_fusion.4
  299.3 100.8 %psum.30 = f32[16]{0:T(128)S(1)} all-reduce(f32[16]{0:T(128)S(1)} %multiply_reduce_fusion.4), channel_id=1, replica_groups=mesh['row'=32,'col'=16] {'row','col'}, use_global_device_ids=true, to_apply=%region_10.0 | all-reduce | flops 16 | bytes 128 | tf_op jit(solution)/shard_map/psum | solution.py:65
  400.3 28.5 %all-gather.1 = f32[32,64,16]{1,2,0:T(8,128)S(1)} all-gather(f32[1,64,16]{1,2,0:T(8,128)S(1)} %fusion.105), channel_id=1, replica_groups=mesh['row'=32,'col'=16] {'row'}, dimensions={0}, use_global_device_ids=true | all-gather | bytes 135168 | tf_op jit(solution)/shard_map/all_gather | solution.py:74
  428.8 0.1 copy.25
  428.9 0.1 reshape.18
  429.0 11.9 %while.43 = (s32[]{:T(128)}, f32[16,1024]{1,0:T(8,128)S(1)}, f32[16,2048]{1,0:T(8,128)S(1)}, f32[2048]{0:T(1024)S(1)}, f32[1024]{0:T(1024)S(1)}, /*index=5*/bf16...) while((s32[]{:T(128)}, f32[16,1024]{1,0:T(8,128)S(1)}, ...), condition=%wide.region_12.0_spmd.clone, body=%wide.region_11.0_spmd.clone.sunk | while | flops 173047808 | bytes 4565169 | solution.py:45
  429.0 0.5 fusion.137
  429.5 2.4 fusion.138
  432.0 0.5 fusion.137
  432.5 2.4 fusion.138
  435.0 0.5 fusion.137
  435.5 2.4 fusion.138
  437.9 0.5 fusion.137
  438.5 2.4 fusion.138
  440.9 1.0 copy.34
  442.0 22.1 %all_gather.23 = bf16[64,1024]{0,1:T(8,128)(2,1)S(1)} all-gather(bf16[64,64]{0,1:T(8,128)(2,1)S(1)} %get-tuple-element.537), channel_id=1, replica_groups=mesh['row'=32,'col'=16] {'col'}, dimensions={1}, use_global_device_ids=true | all-gather | bytes 139264 | tf_op jit(solution)/shard_map/all_gather | solution.py:53
  464.1 0.1 copy.31
  464.2 0.2 multiply_reduce_fusion.1
  464.4 60.8 %reduce-scatter.12.cloned.1.call-done = f32[64,16]{1,0:T(8,128)} async-done(((f32[1024,16]{1,0:T(8,128)}), f32[64,16]{1,0:T(8,128)}) %reduce-scatter.12.cloned.1.call-update) | async-done | bytes 4112
  525.2 0.8 copy.35
  526.0 0.2 multiply_reduce_fusion.3
  526.2 102.1 %psum.31 = f32[16]{0:T(128)S(1)} all-reduce(f32[16]{0:T(128)S(1)} %multiply_reduce_fusion.3), channel_id=1, replica_groups=mesh['row'=32,'col'=16] {'row','col'}, use_global_device_ids=true, to_apply=%region_15.0 | all-reduce | flops 16 | bytes 128 | tf_op jit(solution)/shard_map/psum | solution.py:78
  628.4 28.8 %all-gather.2 = f32[32,64,16]{1,2,0:T(8,128)S(1)} all-gather(f32[1,64,16]{1,2,0:T(8,128)S(1)} %bitcast.44), channel_id=1, replica_groups=mesh['row'=32,'col'=16] {'row'}, dimensions={0}, use_global_device_ids=true | all-gather | bytes 135168 | tf_op jit(solution)/shard_map/all_gather | solution.py:86
  657.2 0.1 copy.28
  657.3 0.1 reshape.20
  657.4 11.9 %while.44 = (s32[]{:T(128)}, f32[16,1024]{1,0:T(8,128)S(1)}, f32[16,2048]{1,0:T(8,128)S(1)}, f32[2048]{0:T(1024)S(1)}, f32[1024]{0:T(1024)S(1)}, /*index=5*/bf16...) while((s32[]{:T(128)}, f32[16,1024]{1,0:T(8,128)S(1)}, ...), condition=%wide.region_18.0_spmd.clone, body=%wide.region_17.0_spmd.clone.sunk | while | flops 173047808 | bytes 4565169 | solution.py:45
  657.4 0.5 fusion.143
  658.0 2.4 fusion.144
  660.4 0.5 fusion.143
  660.9 2.4 fusion.144
  663.4 0.5 fusion.143
  663.9 2.4 fusion.144
  666.3 0.5 fusion.143
  666.9 2.4 fusion.144
  669.3 1.0 copy.36
  670.3 85.4 %reduce-scatter.14.cloned.1.call-done = f32[64,16]{1,0:T(8,128)} async-done(((f32[1024,16]{1,0:T(8,128)}), f32[64,16]{1,0:T(8,128)}) %reduce-scatter.14.cloned.1.call-update) | async-done | bytes 4112
  755.7 1.4 copy.37
  (31 shorter events, 1.2 us)
Async XLA Ops:
  7.2 64.7 %copy-start = (f32[16,64]{1,0:T(8,128)S(1)}, f32[16,64]{1,0:T(8,128)}, u32[]{:S(2)}) copy-start(f32[16,64]{1,0:T(8,128)} %param.15) | copy-start | bytes 12292
  7.2 189.2 %reduce-scatter.10.cloned.1.call-start = ((), (), s32[]{:S(2)}) async-start(), calls=%async_computation.3 | async-start | bytes 557056
  99.6 97.6 %copy-start.2 = (f32[64]{0:T(128)S(1)}, f32[64]{0:T(128)}, u32[]{:S(2)}) copy-start(f32[64]{0:T(128)} %param.14) | copy-start | bytes 772
  112.6 412.6 %reduce-scatter.12.cloned.1.call-start = ((), (), s32[]{:S(2)}) async-start(), calls=%async_computation.4 | async-start | bytes 557056
  441.9 313.8 %reduce-scatter.14.cloned.1.call-start = ((), (), s32[]{:S(2)}) async-start(), calls=%async_computation.5 | async-start | bytes 557056
  628.4 29.0 %copy-start.1 = (f32[16,64]{1,0:T(8,128)}, f32[16,64]{1,0:T(8,128)S(1)}, u32[]{:S(2)}) copy-start(f32[16,64]{1,0:T(8,128)S(1)} %multiply_add_fusion) | copy-start | bytes 12292
Sparse Core Ops, SparseCore 0:
  112.7 83.6 reduce-scatter.9
  442.1 83.1 reduce-scatter.11
  670.5 85.2 reduce-scatter.13
where the time goes:
time: 764 us
  blocking collectives  473 us (62%)
  waiting for transfers between devices  230 us (30%)
  matrix products  34.7 us (5%)
  between operations  13.9 us (2%)
  local copies, waits for them, and re-layouts  9.77 us (1%)
    unnamed x6, waiting for transfers between devices  230 us
    psum x2, blocking collectives, squares(): return lax.psum(jnp.sum(residual * residual, axis=1), ('row', 'col'))  203 us
    psum x1, blocking collectives, per_device(): lax.psum(jnp.sum(direction * image, axis=1), ('row', 'col'))  102 us
    all_gather x2, blocking collectives, per_device(): lax.all_gather(direction, 'row', axis=1, tiled=True)  56 us
    all_gather x1, blocking collectives, per_device(): col_train = lax.all_gather(scaled_train, 'row', axis=1, tiled=True)  37.6 us
    dot_general x12, matrix products, advance(): jnp.dot(sub_vector, kernel_tile, precision=lax.Precision.HIGHEST, preferr...  29.1 us
    all_gather x1, blocking collectives, per_device(): lax.all_gather(solution, 'row', axis=1, tiled=True)  28.8 us
    all_gather x1, blocking collectives, per_device(): lax.all_gather(scaled_train, 'col', axis=1, tiled=True)  23.8 us
  transfers between devices with their start and end apart: 3, of which 3 were waited for; matrix products, arithmetic and copies ran while one was open for 0% of the time, Pallas kernels for 0%

commit v1 on v0

--- a/solution.py
+++ b/solution.py
@@ -83,7 +83,12 @@
         norm_now = norm_next
     mean_start = jnp.zeros((outputs, row_cand.shape[1]), jnp.float32)
     partial_mean = from_columns(
-        row_cand, cand_norms, mean_start, lax.all_gather(solution, "row", axis=1, tiled=True)
+        row_cand,
+        cand_norms,
+        mean_start,
+        jnp.concatenate(
+            lax.all_to_all(jnp.stack([solution] * lax.axis_size("row")), "row", 0, 0), axis=1
+        ),
     )
     post_mean = lax.psum_scatter(partial_mean, "col", scatter_dimension=1, tiled=True)
     return (solution, post_mean)

time: 764 us -> 774 us (1.013)
  blocking collectives: 473 us -> 446 us
  waiting for transfers between devices: 230 us -> 255 us
  starting transfers between devices: 0.12 us -> 9.07 us
    all_gather x1 -> x0, blocking collectives: 28.8 us -> none  [per_device(): lax.all_gather(solution, 'row', axis=1, tiled=True)]
    unnamed x6, waiting for transfers between devices: 230 us -> 255 us
    all_to_all x0 -> x1, starting transfers between devices: none -> 8.95 us  [per_device(): lax.all_to_all(jnp.stack([solution] * lax.axis_size('row')), 'row', 0, 0)]
  transfers between devices with their start and end apart: 3 -> 4, of which waited for: 3 -> 3; matrix products, arithmetic and copies ran while one was open for 0% -> 0% of each run, Pallas kernels for 0% -> 0%
where the time goes in v1:
time: 774 us; the launch traced here: 773 us
  blocking collectives  446 us (58%)
  waiting for transfers between devices  255 us (33%)
  matrix products  34.7 us (4%)
  between operations  13.9 us (2%)
  local copies, waits for them, and re-layouts  11.3 us (1%)
  starting transfers between devices  9.07 us (1%)
    unnamed x6, waiting for transfers between devices  255 us
    psum x2, blocking collectives, squares(): return lax.psum(jnp.sum(residual * residual, axis=1), ('row', 'col'))  203 us
    psum x1, blocking collectives, per_device(): lax.psum(jnp.sum(direction * image, axis=1), ('row', 'col'))  102 us
    all_gather x2, blocking collectives, per_device(): lax.all_gather(direction, 'row', axis=1, tiled=True)  56.1 us
    all_gather x1, blocking collectives, per_device(): col_train = lax.all_gather(scaled_train, 'row', axis=1, tiled=True)  37.6 us
    dot_general x12, matrix products, advance(): jnp.dot(sub_vector, kernel_tile, precision=lax.Precision.HIGHEST, preferr...  29.1 us
    all_gather x1, blocking collectives, per_device(): lax.all_gather(scaled_cand, 'col', axis=1, tiled=True)  23.8 us
    all_gather x1, blocking collectives, per_device(): lax.all_gather(scaled_train, 'col', axis=1, tiled=True)  23.8 us
  transfers between devices with their start and end apart: 4, of which 3 were waited for; matrix products, arithmetic and copies ran while one was open for 0% of the time, Pallas kernels for 0%

profile of v1, /device:TPU:2, one launch (start us, length us, event | category | flops | bytes accessed | tf_op | source)
XLA Modules:
  0.0 772.8 jit_solution(12190338384079899961)
XLA Ops:
  7.2 0.8 copy.20
  8.1 0.8 copy.27
  8.9 0.7 multiply_convert_fusion
  9.6 37.6 %all_gather.16 = bf16[64,2048]{0,1:T(8,128)(2,1)S(1)} all-gather(bf16[64,64]{0,1:T(8,128)(2,1)S(1)} %get-tuple-element.538), channel_id=1, replica_groups=mesh['row'=32,'col'=16] {'row'}, dimensions={1}, use_global_device_ids=true | all-gather | bytes 270336 | tf_op jit(solution)/shard_map/all_gather | solution.py:55
  47.2 0.2 copy.21
  47.4 0.3 multiply_reduce_fusion
  47.8 23.8 %all_gather.17 = bf16[64,1024]{0,1:T(8,128)(2,1)S(1)} all-gather(bf16[64,64]{0,1:T(8,128)(2,1)S(1)} %get-tuple-element.538), channel_id=1, replica_groups=mesh['row'=32,'col'=16] {'col'}, dimensions={1}, use_global_device_ids=true | all-gather | bytes 139264 | tf_op jit(solution)/shard_map/all_gather | solution.py:52
  71.5 0.1 copy.22
  71.7 0.2 multiply_reduce_fusion.2
  71.9 27.5 %all-gather = f32[32,64,16]{1,2,0:T(8,128)S(1)} all-gather(f32[1,64,16]{1,2,0:T(8,128)S(1)} %bitcast.33), channel_id=1, replica_groups=mesh['row'=32,'col'=16] {'row'}, dimensions={0}, use_global_device_ids=true | all-gather | bytes 135168 | tf_op jit(solution)/shard_map/all_gather | solution.py:74
  99.5 0.1 reshape.26
  99.6 11.9 %while.42 = (s32[]{:T(128)}, f32[16,1024]{1,0:T(8,128)S(1)}, f32[16,2048]{1,0:T(8,128)S(1)}, f32[2048]{0:T(1024)S(1)}, f32[1024]{0:T(1024)S(1)}, /*index=5*/bf16...) while((s32[]{:T(128)}, f32[16,1024]{1,0:T(8,128)S(1)}, ...), condition=%wide.region_5.0_spmd.clone, body=%wide.region_4.0_spmd.clone.sunk | while | flops 173047808 | bytes 4565169 | solution.py:45
  99.7 0.5 fusion.131
  100.2 2.4 fusion.132
  102.6 0.5 fusion.131
  103.2 2.4 fusion.132
  105.6 0.5 fusion.131
  106.1 2.4 fusion.132
  108.6 0.5 fusion.131
  109.1 2.4 fusion.132
  111.5 1.0 copy.30
  112.6 83.7 %reduce-scatter.10.cloned.1.call-done = f32[64,16]{1,0:T(8,128)} async-done(((f32[1024,16]{1,0:T(8,128)}), f32[64,16]{1,0:T(8,128)}) %reduce-scatter.10.cloned.1.call-update) | async-done | bytes 4112
  196.4 0.8 copy.31
  197.2 0.1 multiply_reduce_fusion.5
  197.3 101.8 %all-reduce = (f32[16]{0:T(128)S(1)}, f32[16]{0:T(128)S(1)}) all-reduce(f32[16]{0:T(128)S(1)} %get-tuple-element.492, f32[16]{0:T(128)S(1)} %get-tuple-element.491), channel_id=1, replica_groups=mesh['row'=32,'col'=16] {'row','col'}, use_global_device_ids=true, to_apply=%region_1.0 | all-reduce | flops 32 | bytes 256 | tf_op jit(solution)/shard_map/psum | solution.py:65
  299.1 0.2 multiply_reduce_fusion.4
  299.3 100.8 %psum.30 = f32[16]{0:T(128)S(1)} all-reduce(f32[16]{0:T(128)S(1)} %multiply_reduce_fusion.4), channel_id=1, replica_groups=mesh['row'=32,'col'=16] {'row','col'}, use_global_device_ids=true, to_apply=%region_10.0 | all-reduce | flops 16 | bytes 128 | tf_op jit(solution)/shard_map/psum | solution.py:65
  400.2 28.5 %all-gather.1 = f32[32,64,16]{1,2,0:T(8,128)S(1)} all-gather(f32[1,64,16]{1,2,0:T(8,128)S(1)} %fusion.105), channel_id=1, replica_groups=mesh['row'=32,'col'=16] {'row'}, dimensions={0}, use_global_device_ids=true | all-gather | bytes 135168 | tf_op jit(solution)/shard_map/all_gather | solution.py:74
  428.9 0.1 reshape.28
  429.0 11.9 %while.43 = (s32[]{:T(128)}, f32[16,1024]{1,0:T(8,128)S(1)}, f32[16,2048]{1,0:T(8,128)S(1)}, f32[2048]{0:T(1024)S(1)}, f32[1024]{0:T(1024)S(1)}, /*index=5*/bf16...) while((s32[]{:T(128)}, f32[16,1024]{1,0:T(8,128)S(1)}, ...), condition=%wide.region_12.0_spmd.clone, body=%wide.region_11.0_spmd.clone.sunk | while | flops 173047808 | bytes 4565169 | solution.py:45
  429.0 0.5 fusion.137
  429.5 2.4 fusion.138
  432.0 0.5 fusion.137
  432.5 2.4 fusion.138
  434.9 0.5 fusion.137
  435.5 2.4 fusion.138
  437.9 0.5 fusion.137
  438.5 2.4 fusion.138
  440.9 1.0 copy.32
  441.9 83.3 %reduce-scatter.12.cloned.1.call-done = f32[64,16]{1,0:T(8,128)} async-done(((f32[1024,16]{1,0:T(8,128)}), f32[64,16]{1,0:T(8,128)}) %reduce-scatter.12.cloned.1.call-update) | async-done | bytes 4112
  525.2 0.8 copy.33
  526.0 0.2 multiply_reduce_fusion.3
  526.2 101.8 %psum.31 = f32[16]{0:T(128)S(1)} all-reduce(f32[16]{0:T(128)S(1)} %multiply_reduce_fusion.3), channel_id=1, replica_groups=mesh['row'=32,'col'=16] {'row','col'}, use_global_device_ids=true, to_apply=%region_15.0 | all-reduce | flops 16 | bytes 128 | tf_op jit(solution)/shard_map/psum | solution.py:78
  628.2 0.8 reshape.35
  629.0 8.9 %all-to-all-start = ((f32[32,1,1024]{2,1,0:T(1,128)}), f32[32,1,1024]{2,1,0:T(1,128)S(1)}, u32[]{:S(2)}, u32[]{:S(2)}) async-start(f32[32,1,1024]{2,1,0:T(1,128)} %reshape.35), calls=%async_computation | async-start | bytes 262144 | tf_op jit(solution)/shard_map/all_to_all | solution.py:90
  638.0 23.8 %all_gather.19 = bf16[64,1024]{0,1:T(8,128)(2,1)S(1)} all-gather(bf16[64,64]{0,1:T(8,128)(2,1)S(1)} %get-tuple-element.537), channel_id=1, replica_groups=mesh['row'=32,'col'=16] {'col'}, dimensions={1}, use_global_device_ids=true | all-gather | bytes 139264 | tf_op jit(solution)/shard_map/all_gather | solution.py:53
  661.8 0.1 copy.29
  662.0 0.2 multiply_reduce_fusion.1
  662.2 0.6 broadcast.251
  662.8 1.0 reduce
  663.8 0.1 reshape.36
  664.0 0.1 reshape.24
  664.1 11.9 %while.44 = (s32[]{:T(128)}, f32[16,1024]{1,0:T(8,128)S(1)}, f32[16,2048]{1,0:T(8,128)S(1)}, f32[2048]{0:T(1024)S(1)}, f32[1024]{0:T(1024)S(1)}, /*index=5*/bf16...) while((s32[]{:T(128)}, f32[16,1024]{1,0:T(8,128)S(1)}, ...), condition=%wide.region_18.0_spmd.clone, body=%wide.region_17.0_spmd.clone.sunk | while | flops 173047808 | bytes 4565169 | solution.py:45
  664.1 0.5 fusion.143
  664.7 2.4 fusion.144
  667.1 0.5 fusion.143
  667.7 2.4 fusion.144
  670.1 0.5 fusion.143
  670.6 2.4 fusion.144
  673.1 0.5 fusion.143
  673.6 2.4 fusion.144
  676.0 1.0 copy.34
  677.1 87.8 %reduce-scatter.14.cloned.1.call-done = f32[64,16]{1,0:T(8,128)} async-done(((f32[1024,16]{1,0:T(8,128)}), f32[64,16]{1,0:T(8,128)}) %reduce-scatter.14.cloned.1.call-update) | async-done | bytes 4112
  764.8 1.4 copy.35
  (37 shorter events, 1.6 us)
Async XLA Ops:
  7.2 64.7 %copy-start = (f32[16,64]{1,0:T(8,128)S(1)}, f32[16,64]{1,0:T(8,128)}, u32[]{:S(2)}) copy-start(f32[16,64]{1,0:T(8,128)} %param.15) | copy-start | bytes 12292
  7.2 189.2 %reduce-scatter.10.cloned.1.call-start = ((), (), s32[]{:S(2)}) async-start(), calls=%async_computation.4 | async-start | bytes 557056
  99.6 97.6 %copy-start.2 = (f32[64]{0:T(128)S(1)}, f32[64]{0:T(128)}, u32[]{:S(2)}) copy-start(f32[64]{0:T(128)} %param.14) | copy-start | bytes 772
  112.6 412.6 %reduce-scatter.12.cloned.1.call-start = ((), (), s32[]{:S(2)}) async-start(), calls=%async_computation.5 | async-start | bytes 557056
  628.1 36.0 %copy-start.1 = (f32[16,64]{1,0:T(8,128)}, f32[16,64]{1,0:T(8,128)S(1)}, u32[]{:S(2)}) copy-start(f32[16,64]{1,0:T(8,128)S(1)} %multiply_add_fusion) | copy-start | bytes 12292
  629.0 33.2 %all-to-all-start = ((f32[32,1,1024]{2,1,0:T(1,128)}), f32[32,1,1024]{2,1,0:T(1,128)S(1)}, u32[]{:S(2)}, u32[]{:S(2)}) async-start(f32[32,1,1024]{2,1,0:T(1,128)} %reshape.35), calls=%async_computation | async-start | bytes 262144 | tf_op jit(solution)/shard_map/all_to_all | solution.py:90
  637.9 126.9 %reduce-scatter.14.cloned.1.call-start = ((), (), s32[]{:S(2)}) async-start(), calls=%async_computation.6 | async-start | bytes 557056
Sparse Core Ops, SparseCore 0:
  112.7 83.6 reduce-scatter.9
  442.0 83.1 reduce-scatter.11
  677.2 87.5 reduce-scatter.13
